TPU v7x, 32 devices: a whole 2x2x4 slice. The times are simulated.
32 devices in a mesh: island: 4 (over y, x), shard: 8 (over z, core).
Axes of the slice: x: 2, y: 2, z: 4, core: 2. Of those that a mesh axis runs over, the one named last changes fastest.
Arguments:
- gate_pre: bfloat16 [16384, 256], P(('island', 'shard')), may hold values from -6 to 6
- up_pre: bfloat16 [16384, 256], P(('island', 'shard')), may hold values from -6 to 6
- grad_out: bfloat16 [16384, 8192], P(('island', 'shard')), may hold values from -6 to 6
- token_ids: int32 [16384], P(('island', 'shard')), may hold values from 0 to 128255, as said below
- step_count: int32 [1], replicated, may hold values from 0 to 999
- island_drift: float32 [4, 256, 8192], P('island', 'shard'), may hold values from -4 to 4
- adam_m: float32 [4, 256, 8192], P('island', 'shard'), may hold values from -0.015625 to 0.015625
- adam_v: float32 [4, 256, 8192], P('island', 'shard'), may hold values from 3.8146972e-08 to 6.1035155e-07
- anchor: float32 [256, 8192], P('shard'), may hold values from -6 to 6
- momentum: float32 [256, 8192], P('shard'), may hold values from -4 to 4
- next_hidden: bfloat16 [16384, 256], P(('island', 'shard')), may hold values from -6 to 6
Outputs:
- new_anchor: float32 [256, 8192], P('shard', 'island')
- new_momentum: float32 [256, 8192], P('shard', 'island')
- next_out: bfloat16 [16384, 8192], P(('island', 'shard'))
- live_share: float32 [4], P('island')
Inputs may be any that keep to these rules, and one draw needn't show every extreme that they name: `token_ids`: 0 marks padding; within each aligned block of 512 rows the padding comes last, and a third or more of the block's rows are tokens.
All inputs are finite; a program needn't handle non-finite values.
Results may differ from a plain program's by a relative error of at most 0.0004.
The roundings to bfloat16 on the way count: a program that leaves them out, or rounds other values in their place, can miss the bound.
Values may be sent and summed in bfloat16 or wider, within the bound.
A program may use at most 128 MiB of HBM per device.

v0:
```python
import math

import jax
import jax.numpy as jnp
from jax import lax
from jax.sharding import PartitionSpec as P

peak_rate = 0.25
beta_one = 0.9
beta_two = 0.95
adam_eps = 1e-08
decay_rate = 0.1
outer_rate = 0.7
outer_beta = 0.9


def shards(
    gate_pre,
    up_pre,
    grad_out,
    token_ids,
    step_count,
    island_drift,
    adam_m,
    adam_v,
    anchor,
    momentum,
    next_hidden,
):
    row_count = anchor.shape[0]
    width = anchor.shape[1]
    islands = lax.axis_size("island")
    factor = float(row_count * lax.axis_size("shard")) ** (-0.5)
    hidden = (jax.nn.silu(gate_pre.astype(jnp.float32)) * up_pre.astype(jnp.float32)).astype(
        jnp.bfloat16
    )
    live_rows = token_ids != 0
    masked = jnp.where(live_rows[:, None], grad_out, jnp.zeros_like(grad_out))
    tally = lax.psum(jnp.sum(live_rows.astype(jnp.float32)), "shard")
    slot_total = float(token_ids.shape[0] * lax.axis_size("shard"))
    live_share = jnp.reshape(tally / slot_total, (1,))
    columns = hidden
    reduced = lax.psum_scatter(
        lax.dot_general(
            columns, masked, (((0,), (0,)), ((), ())), preferred_element_type=jnp.float32
        )
        * factor,
        "shard",
        scatter_dimension=0,
        tiled=True,
    )
    gradient = reduced / tally
    moment = step_count[0].astype(jnp.float32)
    inner_rate = (
        peak_rate
        * jnp.minimum(1.0, (moment + 1.0) / 100.0)
        * (0.1 + 0.45 * (1.0 + jnp.cos(math.pi * moment / 1000.0)))
    )
    bias_one = 1.0 - jnp.power(jnp.float32(beta_one), moment + 1.0)
    bias_two = 1.0 - jnp.power(jnp.float32(beta_two), moment + 1.0)
    first_moment = beta_one * adam_m[0] + (1.0 - beta_one) * gradient
    second_moment = beta_two * adam_v[0] + (1.0 - beta_two) * gradient * gradient
    direction = first_moment / bias_one / (jnp.sqrt(second_moment / bias_two) + adam_eps)
    params = anchor + island_drift[0]
    updated = params - inner_rate * (direction + decay_rate * params)
    change = anchor - updated
    col_count = width // islands
    col_start = lax.axis_index("island") * col_count
    mean_change = lax.psum(change, "island") / islands
    full_momentum = outer_beta * momentum + mean_change
    full_anchor = anchor - outer_rate * (mean_change + outer_beta * full_momentum)
    weights = full_anchor.astype(jnp.bfloat16)
    new_anchor = lax.dynamic_slice_in_dim(full_anchor, col_start, col_count, 1)
    new_momentum = lax.dynamic_slice_in_dim(full_momentum, col_start, col_count, 1)
    columns = next_hidden
    produced = jnp.dot(
        columns,
        lax.all_gather(weights, "shard", axis=0, tiled=True),
        preferred_element_type=jnp.float32,
    )
    next_out = (produced * factor).astype(jnp.bfloat16)
    return (new_anchor, new_momentum, next_out, live_share)


def solution(mesh):
    in_specs = (
        P(("island", "shard"), None),
        P(("island", "shard"), None),
        P(("island", "shard"), None),
        P(("island", "shard")),
        P(),
        P("island", "shard", None),
        P("island", "shard", None),
        P("island", "shard", None),
        P("shard", None),
        P("shard", None),
        P(("island", "shard"), None),
    )
    out_specs = (
        P("shard", "island"),
        P("shard", "island"),
        P(("island", "shard"), None),
        P("island"),
    )
    return jax.shard_map(shards, mesh=mesh, in_specs=in_specs, out_specs=out_specs, check_vma=False)
```

profile of v0, /device:TPU:1, one launch (start us, length us, event | category | flops | bytes accessed | tf_op | source)
XLA Modules:
  0.0 242.6 jit_solution(4508063332395682022)
XLA Ops:
  7.2 0.0 copy-start
  7.2 0.0 reduce-scatter.2.cloned.1.call-start
  7.2 1.3 convert_reduce_fusion
  8.5 9.5 %convolution_multiply_fusion = f32[256,8192]{1,0:T(8,128)} fusion(bf16[512,8192]{1,0:T(8,128)(2,1)} %param.13, pred[512]{0:T(512)(128)(4,1)S(1)} %get-tuple-element.11, bf16[512,256]{1,0:T(8,128)(2,1)} %param.12, bf16[512,256]{1,0:T(8,128)(2,1)} %param.11), kind=kOutput, calls=%fused_computation.2 | convolution fusion | flops 2154823680 | bytes 17302016 | tf_op jit(solution)/shard_map/dot_general | solution.py:44
  18.0 0.0 copy-start.1
  18.0 0.0 copy-start.2
  18.0 0.0 copy-start.3
  18.0 0.0 reduce-scatter.2.cloned.1.call-update
  18.1 0.0 all-reduce.2.cloned.1.call-start
  18.1 15.5 %psum.14 = f32[]{:T(128)} all-reduce(f32[]{:T(128)} %get-tuple-element.10), channel_id=1, replica_groups=mesh['island'=4,'shard'=8] {'shard'}, use_global_device_ids=true, to_apply=%region_2.3 | all-reduce | flops 1 | bytes 8 | tf_op jit(solution)/shard_map/psum | solution.py:39
  34.5 73.7 %reduce-scatter.2.cloned.1.call-done = f32[32,8192]{1,0:T(8,128)} async-done(((f32[256,8192]{1,0:T(8,128)}), f32[32,8192]{1,0:T(8,128)}) %reduce-scatter.2.cloned.1.call-update) | async-done | bytes 1048592 | tf_op jit(solution)/shard_map/reduce_scatter | solution.py:43
  108.2 0.0 copy-done.1
  108.2 0.0 copy-done.2
  108.2 0.0 copy-done.3
  108.2 4.1 %subtract_subtract_fusion = f32[32,8192]{1,0:T(8,128)} fusion(f32[32,8192]{1,0:T(8,128)S(1)} %copy-done.1, f32[1,32,8192]{2,1,0:T(8,128)S(1)} %copy-done.2, f32[1,32,8192]{2,1,0:T(8,128)S(1)} %copy-done.3, f32[32,8192]{1,0:T(8,128)} %reduce-scatter.2.cloned.1.call-done, f32[1,32,8192]{2,1,0:T(8,128)} %param.17, f32[]{:T(128)} %bitcast.5, f32[]{:T(128)} %bitcast.3, ...), kind=kLoop, calls=%fused_computation.17 | loop fusion | flops 4718592 | bytes 6291472 | tf_op jit(solution)/shard_map/sub | solution.py:66
  112.2 0.0 all-reduce.2.cloned.1.call-update
  112.2 0.0 all-gather.2.cloned.1.call-start
  112.3 52.7 %all-reduce.2.cloned.1.call-done = f32[32,8192]{1,0:T(8,128)} async-done(((f32[32,8192]{1,0:T(8,128)}), f32[32,8192]{1,0:T(8,128)}) %all-reduce.2.cloned.1.call-update) | async-done | bytes 1048592 | tf_op jit(solution)/shard_map/psum | solution.py:69
  165.0 2.6 %fusion.19 = (bf16[32,8192]{1,0:T(8,128)(2,1)}, f32[32,8192]{1,0:T(8,128)S(1)}, f32[32,8192]{1,0:T(8,128)S(1)}) fusion(f32[32,8192]{1,0:T(8,128)S(1)} %copy-done.1, f32[32,8192]{1,0:T(8,128)} %param.20, f32[32,8192]{1,0:T(8,128)} %all-reduce.2.cloned.1.call-done), kind=kLoop, calls=%fused_computation.32 | loop fusion | flops 2097152 | bytes 5767168 | tf_op jit(solution)/shard_map/convert_element_type | solution.py:72
  167.6 0.0 all-gather.2.cloned.1.call-update
  168.3 0.8 constant_dynamic-slice_fusion
  169.1 46.1 %all-gather.2.cloned.1.call-done = bf16[256,8192]{1,0:T(8,128)(2,1)} async-done(((bf16[32,8192]{1,0:T(8,128)(2,1)}), bf16[256,8192]{1,0:T(8,128)(2,1)}) %all-gather.2.cloned.1.call-update) | async-done | bytes 4194320 | tf_op jit(solution)/shard_map/all_gather | solution.py:78
  215.2 0.0 copy-done
  215.2 7.8 %fusion = bf16[512,8192]{0,1:T(8,128)(2,1)} fusion(bf16[256,8192]{1,0:T(8,128)(2,1)} %all-gather.2.cloned.1.call-done, bf16[512,256]{1,0:T(8,128)(2,1)S(1)} %copy-done), kind=kOutput, calls=%fused_computation.1 | convolution fusion | flops 2155872256 | bytes 12845056 | tf_op jit(solution)/shard_map/dot_general | solution.py:76
  223.0 11.9 %copy.15 = bf16[512,8192]{1,0:T(8,128)(2,1)} copy(bf16[512,8192]{0,1:T(8,128)(2,1)} %fusion) | data formatting | bytes 16777216
Async XLA Ops:
  7.2 208.0 %copy-start = (bf16[512,256]{1,0:T(8,128)(2,1)S(1)}, bf16[512,256]{1,0:T(8,128)(2,1)}, u32[]{:S(2)}) copy-start(bf16[512,256]{1,0:T(8,128)(2,1)} %param.21) | copy-start | bytes 786436
  7.2 101.0 %reduce-scatter.2.cloned.1.call-start = ((), (), s32[]{:S(2)}) async-start(), calls=%async_computation.1 | async-start | bytes 9437184 | tf_op jit(solution)/shard_map/reduce_scatter | solution.py:43
  18.0 90.1 %copy-start.1 = (f32[32,8192]{1,0:T(8,128)S(1)}, f32[32,8192]{1,0:T(8,128)}, u32[]{:S(2)}) copy-start(f32[32,8192]{1,0:T(8,128)} %param.19) | copy-start | bytes 3145732
  18.0 90.1 %copy-start.2 = (f32[1,32,8192]{2,1,0:T(8,128)S(1)}, f32[1,32,8192]{2,1,0:T(8,128)}, u32[]{:S(2)}) copy-start(f32[1,32,8192]{2,1,0:T(8,128)} %param.16) | copy-start | bytes 3145732
  18.0 90.1 %copy-start.3 = (f32[1,32,8192]{2,1,0:T(8,128)S(1)}, f32[1,32,8192]{2,1,0:T(8,128)}, u32[]{:S(2)}) copy-start(f32[1,32,8192]{2,1,0:T(8,128)} %param.18) | copy-start | bytes 3145732
  18.1 146.9 %all-reduce.2.cloned.1.call-start = ((), (), s32[]{:S(2)}) async-start(), calls=%async_computation.2 | async-start | bytes 2097152 | tf_op jit(solution)/shard_map/psum | solution.py:69
  112.2 103.0 %all-gather.2.cloned.1.call-start = ((), (), s32[]{:S(2)}) async-start(), calls=%async_computation.3 | async-start | bytes 4718592 | tf_op jit(solution)/shard_map/all_gather | solution.py:78
Sparse Core Ops, SparseCore 0:
  18.2 89.9 reduce-scatter.1
  112.4 52.5 all-reduce.1
  167.7 47.4 all-gather.1
where the time goes:
time: 243 us
  waiting for transfers between devices  173 us (71%)
  matrix products  17.3 us (7%)
  between operations  16.4 us (7%)
  blocking collectives  15.5 us (6%)
  local copies, waits for them, and re-layouts  12.8 us (5%)
  other arithmetic  8 us (3%)
    reduce_scatter x1, waiting for transfers between devices, shards(): lax.psum_scatter(lax.dot_general(columns, masked, (((0,), (0,)), ((), ())...  73.7 us
    psum x1, waiting for transfers between devices, shards(): mean_change = lax.psum(change, 'island') / islands  52.7 us
    all_gather x1, waiting for transfers between devices, shards(): lax.all_gather(weights, 'shard', axis=0, tiled=True)  46.1 us
    psum x1, blocking collectives, shards(): tally = lax.psum(jnp.sum(live_rows.astype(jnp.float32)), 'shard')  15.5 us
    unnamed x9, local copies, waits for them, and re-layouts  11.9 us
    dot_general x1, matrix products, shards(): lax.dot_general(columns, masked, (((0,), (0,)), ((), ())), preferred_elem...  9.47 us
    dot_general x1, matrix products, shards(): jnp.dot(columns, lax.all_gather(weights, 'shard', axis=0, tiled=True), pr...  7.81 us
  transfers between devices with their start and end apart: 3, of which 3 were waited for; matrix products, arithmetic and copies ran while one was open for 0% of the time, Pallas kernels for 0%

commit v1 on v0

v1 whole, which is shorter than its diff:
```python
import functools
import math

import jax
import jax.numpy as jnp
from jax import lax
from jax.experimental import pallas as pl
from jax.experimental.pallas import tpu as pltpu
from jax.sharding import PartitionSpec as P

peak_rate = 0.25
beta_one = 0.9
beta_two = 0.95
adam_eps = 1e-08
decay_rate = 0.1
outer_rate = 0.7
outer_beta = 0.9

MESH = pl.DeviceIdType.MESH
CORES = 2


def exchange(
    n_shard, n_island, chunks, wide, factor, slot_total,
    scal, gate, up, tok, gout, drift, adam_m, adam_v, anchor, mom,
    w_out, na_out, nm_out, share_out,
    h_t, g_buf, d_buf, m_buf, v_buf, a_buf, o_buf,
    own, p_send, p_recv, recv,
    x_send, x_recv, w_buf, cnt, tal,
    g_sem, s_sem, o_sem, p_s, p_r, f_s, f_r,
    x_s, x_r, a_s, a_r, b_s, b_r, c_s, c_r, t_s, t_r, out_sem,
):
    chips = n_shard // CORES
    rows = anchor.shape[0]
    shard = lax.axis_index("shard")
    island = lax.axis_index("island")
    chip = shard // CORES
    core = shard % CORES
    span = chunks * wide

    def at(sh, isl):
        return {"shard": sh, "island": isl}

    def remote(src, dst, ss, rs, sh, isl):
        return pltpu.make_async_remote_copy(
            src_ref=src, dst_ref=dst, send_sem=ss, recv_sem=rs,
            device_id=at(sh, isl), device_id_type=MESH)

    def columns(c, i):
        return pl.ds(pl.multiple_of(i * span + c * wide, wide), wide)

    def load_g(c, i):
        return pltpu.make_async_copy(gout.at[:, columns(c, i)], g_buf.at[c, i], g_sem.at[c, i])

    def load_state(c, i):
        col = columns(c, i)
        return [
            pltpu.make_async_copy(src, dst.at[c, i], s_sem.at[j, c, i])
            for j, (src, dst) in enumerate((
                (drift.at[0, :, col], d_buf), (adam_m.at[0, :, col], m_buf),
                (adam_v.at[0, :, col], v_buf), (anchor.at[:, col], a_buf)))
        ]

    def load_mom(c):
        return pltpu.make_async_copy(mom.at[:, columns(c, island)], o_buf.at[c], o_sem.at[c])

    def each(total, body):
        lax.fori_loop(0, total, lambda j, _: (body(j), 0)[1], 0)

    each(chunks, lambda c: each(n_island, lambda i: load_g(c, i).start()))

    def start_state(c):
        each(n_island, lambda i: [cp.start() for cp in load_state(c, i)])
        load_mom(c).start()

    each(chunks, start_state)

    barrier = pltpu.get_barrier_semaphore()
    for off in range(1, n_shard):
        pl.semaphore_signal(barrier, inc=1, device_id=at((shard + off) % n_shard, island), device_id_type=MESH)
    for off in range(1, n_island):
        pl.semaphore_signal(barrier, inc=1, device_id=at(shard, (island + off) % n_island), device_id_type=MESH)

    pre = gate[...].astype(jnp.float32)
    hidden = (pre / (1.0 + jnp.exp(-pre))) * up[...].astype(jnp.float32)
    live = tok[...] != 0
    turned = jnp.where(live, hidden.T, 0.0).astype(jnp.bfloat16)
    for z in range(chips):
        for b in range(CORES):
            h_t[b, pl.ds(z * rows, rows), :] = turned[(z * CORES + b) * rows:(z * CORES + b + 1) * rows]
    cnt[...] = jnp.full(cnt.shape, jnp.sum(live.astype(jnp.float32)), jnp.float32)

    pl.semaphore_wait(barrier, n_shard - 1 + n_island - 1)

    def count_copy(off):
        return remote(cnt, tal.at[off], t_s.at[off], t_r.at[off], (shard + off) % n_shard, island)

    for off in range(1, n_shard):
        count_copy(off).start()

    partner = chip * CORES + (1 - core)

    def pair_copy(c):
        return remote(p_send.at[c], p_recv.at[c], p_s.at[c], p_r.at[c], partner, island)

    def right_copy(c, d):
        return remote(own.at[c, d], recv.at[c, d], f_s.at[c, d], f_r.at[c, d],
                      lax.rem(shard + CORES, n_shard), island)

    def left_copy(c, d):
        slot = jnp.where(d == chip - 1, chips, d)
        return remote(own.at[c, d], recv.at[c, slot], f_s.at[c, d], f_r.at[c, slot],
                      lax.rem(shard + n_shard - CORES, n_shard), island)

    def change_copy(c, off):
        j = (island + off) % n_island
        return remote(x_send.at[c, j], x_recv.at[c, off], x_s.at[c, off], x_r.at[c, off], shard, j)

    def line_copy(c, off):
        to = ((chip + off) % chips) * CORES + core
        mine = w_buf.at[c, island, chip, core]
        return remote(mine, mine, a_s.at[c, off], a_r.at[c, off], to, island)

    def island_copy(c, off):
        mine = w_buf.at[c, island, :, core]
        return remote(mine, mine, b_s.at[c, off], b_r.at[c, off], shard, (island + off) % n_island)

    def core_copy(c):
        mine = w_buf.at[c, :, :, core]
        return remote(mine, mine, c_s.at[c], c_r.at[c], partner, island)

    def store_copy(c):
        return pltpu.make_async_copy(w_buf.at[c], w_out.at[c], out_sem.at[c])

    def within(c, body):
        @pl.when((c >= 0) & (c < chunks))
        def _():
            body(c)

    def product(c):
        def piece(i):
            load_g(c, i).wait()
            g = g_buf[c, i]
            away = jnp.dot(h_t[1 - core], g, preferred_element_type=jnp.float32) * factor
            for d in range(chips):
                p_send[c, d, i] = away[d * rows:(d + 1) * rows]
            here = jnp.dot(h_t[core], g, preferred_element_type=jnp.float32) * factor
            for d in range(chips):
                own[c, d, i] = here[d * rows:(d + 1) * rows]

        each(n_island, piece)
        pair_copy(c).start()

    def add_pair(c):
        pair_copy(c).wait_recv()

        def piece(d):
            own[c, d] = own[c, d] + p_recv[c, d]

        each(chips, piece)

    def arrived(c, slot, d):
        remote(own.at[c, d], recv.at[c, slot], f_s.at[c, d], f_r.at[c, slot], partner, island).wait_recv()
        own[c, d] = own[c, d] + recv[c, slot]

    def flow(c, copy, order, first, ahead):
        for d in order:
            @pl.when(ahead(d))
            def _():
                @pl.when(jnp.logical_not(first))
                def _():
                    arrived(c, d, d)

                copy(c, d).start()

    def right(c):
        flow(c, right_copy, range(chips - 1, -1, -1), chip == 0, lambda d: d > chip)

    def left(c):
        flow(c, left_copy, range(chips), chip == chips - 1, lambda d: d < chip)

    def inner(c):
        @pl.when(chip > 0)
        def _():
            arrived(c, chip, chip)

        @pl.when(chip < chips - 1)
        def _():
            arrived(c, chips, chip)

        tally = cnt[0:1, 0:1]
        for off in range(1, n_shard):
            tally = tally + tal[off, 0:1, 0:1]
        rate, bias_one, bias_two = scal[0], scal[1], scal[2]

        def piece(i):
            for cp in load_state(c, i):
                cp.wait()
            gradient = own[c, chip, i] / tally
            first = beta_one * m_buf[c, i] + (1.0 - beta_one) * gradient
            second = beta_two * v_buf[c, i] + (1.0 - beta_two) * gradient * gradient
            direction = first / bias_one / (jnp.sqrt(second / bias_two) + adam_eps)
            held = a_buf[c, i]
            params = held + d_buf[c, i]
            updated = params - rate * (direction + decay_rate * params)
            x_send[c, i] = held - updated

        each(n_island, piece)
        for off in range(1, n_island):
            change_copy(c, off).start()

    def outer(c):
        total = x_send[c, island]
        for off in range(1, n_island):
            change_copy(c, off).wait_recv()
            total = total + x_recv[c, off]
        mean = total / n_island
        load_mom(c).wait()
        momentum = outer_beta * o_buf[c] + mean
        fresh = a_buf[c, island] - outer_rate * (mean + outer_beta * momentum)
        nm_out[c] = momentum
        na_out[c] = fresh
        w_buf[c, island, chip, core] = fresh.astype(jnp.bfloat16)
        for off in range(1, chips):
            line_copy(c, off).start()

    def spread(c):
        for off in range(1, chips):
            line_copy(c, off).wait_recv()
        for off in range(1, n_island):
            island_copy(c, off).start()

    def pair_up(c):
        for off in range(1, n_island):
            island_copy(c, off).wait_recv()
        core_copy(c).start()

    def finish(c):
        core_copy(c).wait_recv()
        store_copy(c).start()

    def step(t):
        within(t, product)
        within(t - 1, add_pair)
        within(t - 1 - chip, right)
        within(t - 1 - (chips - 1 - chip), left)

        @pl.when(t == chips)
        def _():
            for off in range(1, n_shard):
                count_copy(off).wait_recv()

        within(t - chips, inner)
        within(t - chips - 1, outer)
        within(t - chips - 2, spread)
        within(t - chips - 3, pair_up)
        within(t - chips - 4, finish)

    each(chunks + chips + 4, step)

    tally = cnt[...]
    for off in range(1, n_shard):
        tally = tally + tal[off]
    share_out[...] = tally / slot_total

    for off in range(1, n_shard):
        count_copy(off).wait_send()

    def drain(c):
        pair_copy(c).wait_send()
        for d in range(chips):
            @pl.when(d > chip)
            def _():
                right_copy(c, d).wait_send()

            @pl.when(d < chip)
            def _():
                left_copy(c, d).wait_send()
        for off in range(1, n_island):
            change_copy(c, off).wait_send()
            island_copy(c, off).wait_send()
        for off in range(1, chips):
            line_copy(c, off).wait_send()
        core_copy(c).wait_send()
        store_copy(c).wait()

    each(chunks, drain)


def forward(chunks, wide, factor, nh, w, na, nm, share, out, na_out, nm_out, share_out):
    @pl.when(pl.program_id(0) == 0)
    def _():
        for c in range(chunks):
            na_out[:, c * wide:(c + 1) * wide] = na[c]
            nm_out[:, c * wide:(c + 1) * wide] = nm[c]
        share_out[...] = share[...]

    pair = 2 if chunks % 2 == 0 else 1
    for c in range(0, chunks, pair):
        block = jnp.concatenate(
            [w[c + j, 0].reshape(nh.shape[1], wide) for j in range(pair)], axis=1)
        made = jnp.dot(nh[...], block, preferred_element_type=jnp.float32) * factor
        out[:, c * wide:(c + pair) * wide] = made.astype(jnp.bfloat16)


def shards(
    n_shard, n_island,
    gate_pre, up_pre, grad_out, token_ids, step_count, island_drift,
    adam_m, adam_v, anchor, momentum, next_hidden,
):
    rows, width = anchor.shape
    tokens, hidden_units = gate_pre.shape
    chips = n_shard // CORES
    span = width // n_island
    wide = min(128, span)
    chunks = span // wide
    factor = float(hidden_units) ** (-0.5)
    slot_total = float(tokens * n_shard)
    moment = step_count[0].astype(jnp.float32)
    rate = (
        peak_rate
        * jnp.minimum(1.0, (moment + 1.0) / 100.0)
        * (0.1 + 0.45 * (1.0 + jnp.cos(math.pi * moment / 1000.0)))
    )
    scal = jnp.stack([
        rate,
        1.0 - jnp.power(jnp.float32(beta_one), moment + 1.0),
        1.0 - jnp.power(jnp.float32(beta_two), moment + 1.0),
    ])
    f32, bf16 = jnp.float32, jnp.bfloat16
    any_space = pl.BlockSpec(memory_space=pl.ANY)
    vmem = pl.BlockSpec(memory_space=pltpu.VMEM)
    smem = pl.BlockSpec(memory_space=pltpu.SMEM)
    dma = pltpu.SemaphoreType.DMA
    state = pltpu.VMEM((chunks, n_island, rows, wide), f32)
    lines = pltpu.VMEM((chunks, chips, n_island, rows, wide), f32)
    w_shape = (chunks, n_island, chips, CORES, rows, wide)
    w, na, nm, share = pl.pallas_call(
        functools.partial(exchange, n_shard, n_island, chunks, wide, factor, slot_total),
        out_shape=(
            jax.ShapeDtypeStruct(w_shape, bf16),
            jax.ShapeDtypeStruct((chunks, rows, wide), f32),
            jax.ShapeDtypeStruct((chunks, rows, wide), f32),
            jax.ShapeDtypeStruct((8, 128), f32),
        ),
        in_specs=[smem, vmem, vmem, vmem] + [any_space] * 6,
        out_specs=(any_space, vmem, vmem, vmem),
        scratch_shapes=[
            pltpu.VMEM((CORES, chips * rows, tokens), bf16),
            pltpu.VMEM((chunks, n_island, tokens, wide), bf16),
            state, state, state, state,
            pltpu.VMEM((chunks, rows, wide), f32),
            lines, lines, lines,
            pltpu.VMEM((chunks, chips + 1, n_island, rows, wide), f32),
            state,
            pltpu.VMEM((chunks, n_island, rows, wide), f32),
            pltpu.VMEM(w_shape, bf16),
            pltpu.VMEM((8, 128), f32),
            pltpu.VMEM((n_shard, 8, 128), f32),
            dma((chunks, n_island)), dma((4, chunks, n_island)), dma((chunks,)),
            dma((chunks,)), dma((chunks,)),
            dma((chunks, chips)), dma((chunks, chips + 1)),
            dma((chunks, n_island)), dma((chunks, n_island)),
            dma((chunks, chips)), dma((chunks, chips)),
            dma((chunks, n_island)), dma((chunks, n_island)),
            dma((chunks,)), dma((chunks,)),
            dma((n_shard,)), dma((n_shard,)),
            dma((chunks,)),
        ],
        compiler_params=pltpu.CompilerParams(
            collective_id=0, has_side_effects=True, vmem_limit_bytes=62 * 1024 * 1024),
    )(scal, gate_pre, up_pre, token_ids.reshape(1, tokens), grad_out,
      island_drift, adam_m, adam_v, anchor, momentum)

    def whole(shape):
        return pl.BlockSpec(shape, lambda i: (0,) * len(shape))

    next_out, new_anchor, new_momentum, share = pl.pallas_call(
        functools.partial(forward, chunks, wide, factor),
        grid=(n_island,),
        out_shape=(
            jax.ShapeDtypeStruct((next_hidden.shape[0], width), bf16),
            jax.ShapeDtypeStruct((rows, span), f32),
            jax.ShapeDtypeStruct((rows, span), f32),
            jax.ShapeDtypeStruct((8, 128), f32),
        ),
        in_specs=[
            whole(next_hidden.shape),
            pl.BlockSpec((chunks, 1, chips, CORES, rows, wide), lambda i: (0, i, 0, 0, 0, 0)),
            whole(na.shape), whole(nm.shape), whole(share.shape),
        ],
        out_specs=(
            pl.BlockSpec((next_hidden.shape[0], span), lambda i: (0, i)),
            whole((rows, span)), whole((rows, span)), whole((8, 128)),
        ),
    )(next_hidden, w, na, nm, share)
    return new_anchor, new_momentum, next_out, share[0, 0:1]


def solution(mesh):
    in_specs = (
        P(("island", "shard"), None),
        P(("island", "shard"), None),
        P(("island", "shard"), None),
        P(("island", "shard")),
        P(),
        P("island", "shard", None),
        P("island", "shard", None),
        P("island", "shard", None),
        P("shard", None),
        P("shard", None),
        P(("island", "shard"), None),
    )
    out_specs = (
        P("shard", "island"),
        P("shard", "island"),
        P(("island", "shard"), None),
        P("island"),
    )
    body = functools.partial(shards, mesh.shape["shard"], mesh.shape["island"])
    return jax.shard_map(body, mesh=mesh, in_specs=in_specs, out_specs=out_specs, check_vma=False)
```

time: 243 us -> 124 us (0.51)
  waiting for transfers between devices: 173 us -> 0 us
  Pallas kernels: 0 us -> 121 us
  matrix products: 17.3 us -> 0 us
  blocking collectives: 15.5 us -> 0 us
  between operations: 16.4 us -> 1.45 us
  local copies, waits for them, and re-layouts: 12.8 us -> 1.19 us
  other arithmetic: 8 us -> 0.59 us
    pallas_call x0 -> x2, Pallas kernels: none -> 121 us  [the longest x1 113 us: shards(): pl.pallas_call(functools.partial(exchange, n_shard, n_island, chunks, wid...]
    reduce_scatter x1 -> x0, waiting for transfers between devices: 73.7 us -> none  [shards(): lax.psum_scatter(lax.dot_general(columns, masked, (((0,), (0,)), ((), ())...]
    psum x1 -> x0, waiting for transfers between devices: 52.7 us -> none  [shards(): mean_change = lax.psum(change, 'island') / islands]
    all_gather x1 -> x0, waiting for transfers between devices: 46.1 us -> none  [shards(): lax.all_gather(weights, 'shard', axis=0, tiled=True)]
    dot_general x2 -> x0, matrix products: 17.3 us -> none  [the longest x1 9.47 us: shards(): lax.dot_general(columns, masked, (((0,), (0,)), ((), ())), preferred_elem...]
    psum x1 -> x0, blocking collectives: 15.5 us -> none  [shards(): tally = lax.psum(jnp.sum(live_rows.astype(jnp.float32)), 'shard')]
    unnamed x9 -> x0, local copies, waits for them, and re-layouts: 11.9 us -> none
    sub x1 -> x0, other arithmetic: 4.05 us -> none  [shards(): change = anchor - updated]
  transfers between devices with their start and end apart: 3 -> 0, of which waited for: 3 -> 0; matrix products, arithmetic and copies ran while one was open for 0% -> 0% of each run, Pallas kernels for 0% -> 0%
where the time goes in v1:
time: 124 us
  Pallas kernels  121 us (98%)
  between operations  1.45 us (1%)
    pallas_call x1, Pallas kernels, shards(): pl.pallas_call(functools.partial(exchange, n_shard, n_island, chunks, wid...  113 us
    pallas_call x1, Pallas kernels, shards(): pl.pallas_call(functools.partial(forward, chunks, wide, factor), grid=(n_...  7.38 us

profile of v1, /device:TPU:1, one launch (start us, length us, event | category | flops | bytes accessed | tf_op | source)
XLA Modules:
  0.0 123.9 jit_solution(3690244375740330120)
XLA Ops:
  1.4 0.6 pad_maximum_fusion.scal
  2.0 113.3 %shard_map.138 = (bf16[16,4,4,2,32,128]{5,4,3,2,1,0:T(8,128)(2,1)}, f32[16,32,128]{2,1,0:T(8,128)}, f32[16,32,128]{2,1,0:T(8,128)}, f32[8,128]{1,0:T(8,128)}) custom-call(f32[3]{0:T(128)} %pad_maximum_fusion.scal, bf16[512,256]{1,0:T(8,128)(2,1)} %gate.1, bf16[512,256]{1,0:T(8,128)(2,1)} %up.1, s32[1,512]{1,0:T(1,128)} %bitcast.2, bf16[512,8192]{1,0:T(8,128)(2,1)} %gout.1, ...), custom_call_target="tpu_custom_call" | custom-call | tf_op jit(solution)/shard_map/pallas_call | solution.py:338
  115.4 7.4 %shard_map.139 = (bf16[512,8192]{1,0:T(8,128)(2,1)}, f32[32,2048]{1,0:T(8,128)}, f32[32,2048]{1,0:T(8,128)}, f32[8,128]{1,0:T(8,128)}) custom-call(bf16[512,256]{1,0:T(8,128)(2,1)} %nh.1, bf16[16,4,4,2,32,128]{5,4,3,2,1,0:T(8,128)(2,1)} %get-tuple-element.12.w, f32[16,32,128]{2,1,0:T(8,128)} %get-tuple-element.13.na, f32[16,32,128]{2,1,0:T(8,128)} %get-tuple-element.14.nm, ...), custom_call_target="tpu_custom_call" | custom-call | tf_op jit(solution)/shard_map/pallas_call | solution.py:378
  122.7 1.2 slice.3

commit v2 on v1

--- a/solution.py
+++ b/solution.py
@@ -27,7 +27,7 @@
     h_t, g_buf, d_buf, m_buf, v_buf, a_buf, o_buf,
     own, p_send, p_recv, recv,
     x_send, x_recv, w_buf, cnt, tal,
-    g_sem, s_sem, o_sem, p_s, p_r, f_s, f_r,
+    g_sem, s_sem, p_s, p_r, f_s, f_r,
     x_s, x_r, a_s, a_r, b_s, b_r, c_s, c_r, t_s, t_r, out_sem,
 ):
     chips = n_shard // CORES
@@ -52,28 +52,22 @@
     def load_g(c, i):
         return pltpu.make_async_copy(gout.at[:, columns(c, i)], g_buf.at[c, i], g_sem.at[c, i])
 
-    def load_state(c, i):
-        col = columns(c, i)
-        return [
-            pltpu.make_async_copy(src, dst.at[c, i], s_sem.at[j, c, i])
-            for j, (src, dst) in enumerate((
-                (drift.at[0, :, col], d_buf), (adam_m.at[0, :, col], m_buf),
-                (adam_v.at[0, :, col], v_buf), (anchor.at[:, col], a_buf)))
-        ]
-
-    def load_mom(c):
-        return pltpu.make_async_copy(mom.at[:, columns(c, island)], o_buf.at[c], o_sem.at[c])
+    loads = [
+        pltpu.make_async_copy(src, dst, s_sem.at[j])
+        for j, (src, dst) in enumerate((
+            (drift.at[0], d_buf), (adam_m.at[0], m_buf), (adam_v.at[0], v_buf), (anchor, a_buf),
+            (mom.at[:, pl.ds(pl.multiple_of(island * span, span), span)], o_buf)))
+    ]
 
     def each(total, body):
         lax.fori_loop(0, total, lambda j, _: (body(j), 0)[1], 0)
 
-    each(chunks, lambda c: each(n_island, lambda i: load_g(c, i).start()))
-
-    def start_state(c):
-        each(n_island, lambda i: [cp.start() for cp in load_state(c, i)])
-        load_mom(c).start()
-
-    each(chunks, start_state)
+    def start_g(c):
+        for i in range(n_island):
+            load_g(c, i).start()
+
+    ahead = min(4, chunks)
+    each(ahead, start_g)
 
     barrier = pltpu.get_barrier_semaphore()
     for off in range(1, n_shard):
@@ -88,6 +82,8 @@
     for z in range(chips):
         for b in range(CORES):
             h_t[b, pl.ds(z * rows, rows), :] = turned[(z * CORES + b) * rows:(z * CORES + b + 1) * rows]
+    for cp in loads:
+        cp.start()
     cnt[...] = jnp.full(cnt.shape, jnp.sum(live.astype(jnp.float32)), jnp.float32)
 
     pl.semaphore_wait(barrier, n_shard - 1 + n_island - 1)
@@ -194,14 +190,13 @@
         rate, bias_one, bias_two = scal[0], scal[1], scal[2]
 
         def piece(i):
-            for cp in load_state(c, i):
-                cp.wait()
+            col = columns(c, i)
             gradient = own[c, chip, i] / tally
-            first = beta_one * m_buf[c, i] + (1.0 - beta_one) * gradient
-            second = beta_two * v_buf[c, i] + (1.0 - beta_two) * gradient * gradient
+            first = beta_one * m_buf[:, col] + (1.0 - beta_one) * gradient
+            second = beta_two * v_buf[:, col] + (1.0 - beta_two) * gradient * gradient
             direction = first / bias_one / (jnp.sqrt(second / bias_two) + adam_eps)
-            held = a_buf[c, i]
-            params = held + d_buf[c, i]
+            held = a_buf[:, col]
+            params = held + d_buf[:, col]
             updated = params - rate * (direction + decay_rate * params)
             x_send[c, i] = held - updated
 
@@ -215,9 +210,9 @@
             change_copy(c, off).wait_recv()
             total = total + x_recv[c, off]
         mean = total / n_island
-        load_mom(c).wait()
-        momentum = outer_beta * o_buf[c] + mean
-        fresh = a_buf[c, island] - outer_rate * (mean + outer_beta * momentum)
+        piece = pl.ds(pl.multiple_of(c * wide, wide), wide)
+        momentum = outer_beta * o_buf[:, piece] + mean
+        fresh = a_buf[:, columns(c, island)] - outer_rate * (mean + outer_beta * momentum)
         nm_out[c] = momentum
         na_out[c] = fresh
         w_buf[c, island, chip, core] = fresh.astype(jnp.bfloat16)
@@ -238,33 +233,6 @@
     def finish(c):
         core_copy(c).wait_recv()
         store_copy(c).start()
-
-    def step(t):
-        within(t, product)
-        within(t - 1, add_pair)
-        within(t - 1 - chip, right)
-        within(t - 1 - (chips - 1 - chip), left)
-
-        @pl.when(t == chips)
-        def _():
-            for off in range(1, n_shard):
-                count_copy(off).wait_recv()
-
-        within(t - chips, inner)
-        within(t - chips - 1, outer)
-        within(t - chips - 2, spread)
-        within(t - chips - 3, pair_up)
-        within(t - chips - 4, finish)
-
-    each(chunks + chips + 4, step)
-
-    tally = cnt[...]
-    for off in range(1, n_shard):
-        tally = tally + tal[off]
-    share_out[...] = tally / slot_total
-
-    for off in range(1, n_shard):
-        count_copy(off).wait_send()
 
     def drain(c):
         pair_copy(c).wait_send()
@@ -284,19 +252,56 @@
         core_copy(c).wait_send()
         store_copy(c).wait()
 
-    each(chunks, drain)
-
-
-def forward(chunks, wide, factor, nh, w, na, nm, share, out, na_out, nm_out, share_out):
-    @pl.when(pl.program_id(0) == 0)
+    late = 2
+
+    def step(t):
+        within(t, product)
+        @pl.when(t + ahead < chunks)
+        def _():
+            start_g(t + ahead)
+
+        within(t - 1, add_pair)
+        within(t - 1 - chip, right)
+        within(t - 1 - (chips - 1 - chip), left)
+
+        @pl.when(t == chips)
+        def _():
+            for off in range(1, n_shard):
+                count_copy(off).wait_recv()
+            for cp in loads:
+                cp.wait()
+
+        within(t - chips, inner)
+        within(t - chips - 1, outer)
+        within(t - chips - 2, spread)
+        within(t - chips - 3, pair_up)
+        within(t - chips - 4, finish)
+        within(t - chips - 4 - late, drain)
+
+    each(chunks + chips + 4, step)
+
+    tally = cnt[...]
+    for off in range(1, n_shard):
+        tally = tally + tal[off]
+    share_out[...] = tally / slot_total
+
+    for off in range(1, n_shard):
+        count_copy(off).wait_send()
+
+    each(min(late, chunks), lambda j: drain(chunks - min(late, chunks) + j))
+
+
+def forward(chunks, parts, wide, factor, nh, w, na, nm, share, out, na_out, nm_out, share_out):
+    @pl.when((pl.program_id(0) == 0) & (pl.program_id(1) == 0))
     def _():
         for c in range(chunks):
             na_out[:, c * wide:(c + 1) * wide] = na[c]
             nm_out[:, c * wide:(c + 1) * wide] = nm[c]
-        share_out[...] = share[...]
-
-    pair = 2 if chunks % 2 == 0 else 1
-    for c in range(0, chunks, pair):
+        share_out[0] = share[0, 0]
+
+    count = chunks // parts
+    pair = 2 if count % 2 == 0 else 1
+    for c in range(0, count, pair):
         block = jnp.concatenate(
             [w[c + j, 0].reshape(nh.shape[1], wide) for j in range(pair)], axis=1)
         made = jnp.dot(nh[...], block, preferred_element_type=jnp.float32) * factor
@@ -332,6 +337,7 @@
     vmem = pl.BlockSpec(memory_space=pltpu.VMEM)
     smem = pl.BlockSpec(memory_space=pltpu.SMEM)
     dma = pltpu.SemaphoreType.DMA
+    held = pltpu.VMEM((rows, width), f32)
     state = pltpu.VMEM((chunks, n_island, rows, wide), f32)
     lines = pltpu.VMEM((chunks, chips, n_island, rows, wide), f32)
     w_shape = (chunks, n_island, chips, CORES, rows, wide)
@@ -348,8 +354,8 @@
         scratch_shapes=[
             pltpu.VMEM((CORES, chips * rows, tokens), bf16),
             pltpu.VMEM((chunks, n_island, tokens, wide), bf16),
-            state, state, state, state,
-            pltpu.VMEM((chunks, rows, wide), f32),
+            held, held, held, held,
+            pltpu.VMEM((rows, span), f32),
             lines, lines, lines,
             pltpu.VMEM((chunks, chips + 1, n_island, rows, wide), f32),
             state,
@@ -357,7 +363,7 @@
             pltpu.VMEM(w_shape, bf16),
             pltpu.VMEM((8, 128), f32),
             pltpu.VMEM((n_shard, 8, 128), f32),
-            dma((chunks, n_island)), dma((4, chunks, n_island)), dma((chunks,)),
+            dma((chunks, n_island)), dma((5,)),
             dma((chunks,)), dma((chunks,)),
             dma((chunks, chips)), dma((chunks, chips + 1)),
             dma((chunks, n_island)), dma((chunks, n_island)),
@@ -373,28 +379,30 @@
       island_drift, adam_m, adam_v, anchor, momentum)
 
     def whole(shape):
-        return pl.BlockSpec(shape, lambda i: (0,) * len(shape))
-
-    next_out, new_anchor, new_momentum, share = pl.pallas_call(
-        functools.partial(forward, chunks, wide, factor),
-        grid=(n_island,),
+        return pl.BlockSpec(shape, lambda i, h: (0,) * len(shape))
+
+    parts = 2 if chunks % 2 == 0 else 1
+    count = chunks // parts
+    next_out, new_anchor, new_momentum, live_share = pl.pallas_call(
+        functools.partial(forward, chunks, parts, wide, factor),
+        grid=(n_island, parts),
         out_shape=(
             jax.ShapeDtypeStruct((next_hidden.shape[0], width), bf16),
             jax.ShapeDtypeStruct((rows, span), f32),
             jax.ShapeDtypeStruct((rows, span), f32),
-            jax.ShapeDtypeStruct((8, 128), f32),
+            jax.ShapeDtypeStruct((1,), f32),
         ),
         in_specs=[
             whole(next_hidden.shape),
-            pl.BlockSpec((chunks, 1, chips, CORES, rows, wide), lambda i: (0, i, 0, 0, 0, 0)),
-            whole(na.shape), whole(nm.shape), whole(share.shape),
+            pl.BlockSpec((count, 1, chips, CORES, rows, wide), lambda i, h: (h, i, 0, 0, 0, 0)),
+            whole(na.shape), whole(nm.shape), smem,
         ],
         out_specs=(
-            pl.BlockSpec((next_hidden.shape[0], span), lambda i: (0, i)),
-            whole((rows, span)), whole((rows, span)), whole((8, 128)),
+            pl.BlockSpec((next_hidden.shape[0], count * wide), lambda i, h: (0, i * parts + h)),
+            whole((rows, span)), whole((rows, span)), smem,
         ),
     )(next_hidden, w, na, nm, share)
-    return new_anchor, new_momentum, next_out, share[0, 0:1]
+    return new_anchor, new_momentum, next_out, live_share
 
 
 def solution(mesh):

time: 124 us -> 121 us (0.976)
  Pallas kernels: 121 us -> 118 us
    pallas_call x1, Pallas kernels: 113 us -> 109 us  [shards(): pl.pallas_call(functools.partial(exchange, n_shard, n_island, chunks, wid...]
    pallas_call x1, Pallas kernels: 7.38 us -> 9.15 us  [shards(): pl.pallas_call(functools.partial(forward, chunks, parts, wide, factor), g...]
where the time goes in v2:
time: 121 us
  Pallas kernels  118 us (98%)
  between operations  1.45 us (1%)
    pallas_call x1, Pallas kernels, shards(): pl.pallas_call(functools.partial(exchange, n_shard, n_island, chunks, wid...  109 us
    pallas_call x1, Pallas kernels, shards(): pl.pallas_call(functools.partial(forward, chunks, parts, wide, factor), g...  9.15 us

profile of v2, /device:TPU:1, one launch (start us, length us, event | category | flops | bytes accessed | tf_op | source)
XLA Modules:
  0.0 120.5 jit_solution(12408148403115867684)
XLA Ops:
  1.4 0.6 pad_maximum_fusion.scal
  2.0 109.3 %shard_map.138 = (bf16[16,4,4,2,32,128]{5,4,3,2,1,0:T(8,128)(2,1)}, f32[16,32,128]{2,1,0:T(8,128)}, f32[16,32,128]{2,1,0:T(8,128)}, f32[8,128]{1,0:T(8,128)}) custom-call(f32[3]{0:T(128)} %pad_maximum_fusion.scal, bf16[512,256]{1,0:T(8,128)(2,1)} %gate.1, bf16[512,256]{1,0:T(8,128)(2,1)} %up.1, s32[1,512]{1,0:T(1,128)} %bitcast.1, bf16[512,8192]{1,0:T(8,128)(2,1)} %gout.1, ...), custom_call_target="tpu_custom_call" | custom-call | tf_op jit(solution)/shard_map/pallas_call | solution.py:344
  111.3 9.2 %shard_map.139 = (bf16[512,8192]{1,0:T(8,128)(2,1)}, f32[32,2048]{1,0:T(8,128)}, f32[32,2048]{1,0:T(8,128)}, f32[1]{0:T(128)}) custom-call(bf16[512,256]{1,0:T(8,128)(2,1)} %nh.1, bf16[16,4,4,2,32,128]{5,4,3,2,1,0:T(8,128)(2,1)} %get-tuple-element.12.w, f32[16,32,128]{2,1,0:T(8,128)} %get-tuple-element.13.na, f32[16,32,128]{2,1,0:T(8,128)} %get-tuple-element.14.nm, ...), custom_call_target="tpu_custom_call" | custom-call | tf_op jit(solution)/shard_map/pallas_call | solution.py:386
